TPU v7x, 32 devices: a whole 2x2x4 slice. The times are simulated.
32 devices in a mesh: tile: 8 (over y, x, core), col: 4 (over z).
Axes of the slice: x: 2, y: 2, z: 4, core: 2. Of those that a mesh axis runs over, the one named last changes fastest.
Arguments:
- impedance: bfloat16 [2, 16384, 16384], P(None, 'tile', 'col'), may hold values from -0.0234375 to 0.0234375
- mobility: bfloat16 [256, 64, 128], P('tile'), may hold values from -0.5 to 0.5
- force: bfloat16 [512, 256, 128], P('col', 'tile'), may hold values from -6 to 6
- patch_map: int32 [16384], replicated, may hold values from 0 to 16383, each once
- ownership: int32 [256], P('tile'), may hold values from 0 to 255, each once
Outputs:
- velocity: bfloat16 [512, 256, 128], P('col', 'tile')
- pressure: bfloat16 [512, 2, 16384], P('col', None, 'tile')
Inputs may be any that keep to these rules, and one draw needn't show every extreme that they name: `patch_map`: each patch appears exactly once. `ownership`: each panel appears exactly once.
All inputs are finite; a program needn't handle non-finite values.
Results may differ from a plain program's by a relative error of at most 0.018.
Values may be sent and summed in bfloat16 or wider, within the bound.
A program may use at most 128 MiB of HBM per device.

v0:
```python
import jax
import jax.numpy as jnp
from jax import lax
from jax.sharding import PartitionSpec as P

ITERS = 2


def per_device(impedance, mobility, force, patch_map, ownership):
    imp_re = impedance[0]
    imp_im = impedance[1]
    panel_width = mobility.shape[1]
    slot_count = mobility.shape[0]
    patch_count = patch_map.shape[0]
    loads_dev = force.shape[0]
    col_tiles = lax.axis_size("col")
    col_width = patch_count // col_tiles
    row_width = imp_re.shape[0]
    slot_flat = patch_map.reshape(-1, panel_width)[ownership].reshape(slot_count * panel_width)
    mob_re_t = jnp.transpose(mobility[:, :, :panel_width], (0, 2, 1))
    mob_im_t = jnp.transpose(mobility[:, :, panel_width:], (0, 2, 1))
    upper_rows = jnp.concatenate([mob_re_t, mob_im_t], 2)
    lower_rows = jnp.concatenate([-mob_im_t, mob_re_t], 2)
    real_form = jnp.concatenate([upper_rows, lower_rows], 1)

    def panel_response(drive):
        return jnp.einsum(
            "lsk,skj->lsj", drive, real_form, preferred_element_type=jnp.float32
        ).astype(jnp.bfloat16)

    velocity = panel_response(force)
    pressure = jnp.zeros((loads_dev, 2, row_width), jnp.bfloat16)
    for iteration in range(ITERS):
        values = (
            velocity.reshape(loads_dev, slot_count, 2, panel_width)
            .transpose(0, 2, 1, 3)
            .reshape(loads_dev, 2 * slot_count * panel_width)
        )
        base_pos = slot_flat // col_width * (2 * col_width) + slot_flat % col_width
        flat_index = jnp.concatenate([base_pos, base_pos + col_width])
        placed = jnp.zeros((loads_dev, 2 * patch_count), jnp.bfloat16).at[:, flat_index].set(values)
        placed = placed.reshape(loads_dev, col_tiles, 2, col_width)
        shares = lax.psum_scatter(
            placed.astype(jnp.float32).astype(jnp.bfloat16), "tile", scatter_dimension=3, tiled=True
        )
        moved = lax.all_to_all(shares, "col", split_axis=1, concat_axis=0, tiled=True)
        full_cols = lax.all_gather(moved, "tile", axis=3, tiled=True)
        columns = full_cols.reshape(full_cols.shape[0], 2 * col_width)
        vel_re = columns[:, :col_width]
        vel_im = columns[:, col_width:]
        contract = (((1,), (1,)), ((), ()))

        def dot_rows(left, right):
            return lax.dot_general(left, right, contract, preferred_element_type=jnp.float32)

        real_part = dot_rows(vel_re, imp_re) - dot_rows(vel_im, imp_im)
        imag_part = dot_rows(vel_re, imp_im) + dot_rows(vel_im, imp_re)
        summed = lax.psum_scatter(
            jnp.concatenate([real_part, imag_part], 1).astype(jnp.bfloat16),
            "col",
            scatter_dimension=0,
            tiled=True,
        )
        pressure = summed.reshape(loads_dev, 2, row_width)
        gathered = lax.all_gather(pressure, "tile", axis=2, tiled=True)
        picked = (
            gathered[:, :, slot_flat]
            .reshape(loads_dev, 2, slot_count, panel_width)
            .transpose(0, 2, 1, 3)
            .reshape(loads_dev, slot_count, 2 * panel_width)
        )
        drive = (force.astype(jnp.float32) - picked.astype(jnp.float32)).astype(jnp.bfloat16)
        velocity = panel_response(drive)
    return (velocity, pressure)


def solution(mesh):
    return jax.shard_map(
        per_device,
        mesh=mesh,
        in_specs=(
            P(None, "tile", "col"),
            P("tile", None, None),
            P("col", "tile", None),
            P(),
            P("tile"),
        ),
        out_specs=(P("col", "tile", None), P("col", None, "tile")),
        check_vma=False,
    )
```

profile of v0, /device:TPU:0, one launch (start us, length us, event | category | flops | bytes accessed | tf_op | source)
XLA Modules:
  0.0 846.8 jit_solution(14066625259313548850)
XLA Ops:
  16.3 15.8 %scatter_custom_fusion = bf16[128,32768]{0,1:T(8,128)(2,1)} fusion(s32[4096]{0:T(1024)S(1)} %bitcast.108, bf16[4096,128]{1,0:T(8,128)(2,1)S(1)} %bitcast.101, bf16[]{:T(256)} %constant.36.clone.1), kind=kCustom, calls=%fused_computation.37 | custom fusion | bytes 8388610 | tf_op jit(solution)/shard_map/scatter | solution.py:41
  32.1 11.6 %copy.50 = bf16[128,4,2,4096]{3,0,2,1:T(8,128)(2,1)} copy(bf16[128,4,2,4096]{0,3,2,1:T(8,128)(2,1)} %bitcast.88) | data formatting | bytes 16777216 | tf_op jit(solution)/shard_map/reshape | solution.py:42
  43.8 74.1 %reduce-scatter.5.cloned.1.call-done = bf16[128,4,2,512]{3,0,2,1:T(8,128)(2,1)} async-done(((bf16[128,4,2,4096]{3,0,2,1:T(8,128)(2,1)}), bf16[128,4,2,512]{3,0,2,1:T(8,128)(2,1)}) %reduce-scatter.5.cloned.1.call-update) | async-done | bytes 1048592 | tf_op jit(solution)/shard_map/reduce_scatter | solution.py:43
  117.9 30.1 %all_to_all.36 = bf16[128,4,2,512]{3,0,2,1:T(8,128)(2,1)S(1)} all-to-all(bf16[128,4,2,512]{3,0,2,1:T(8,128)(2,1)} %reduce-scatter.5.cloned.1.call-done), channel_id=1, replica_groups=mesh['tile'=8,'col'=4] {'col'}, dimensions={1} | all-to-all | bytes 2097152 | tf_op jit(solution)/shard_map/all_to_all | solution.py:46
  149.4 53.9 %all-gather.5.cloned.1.call-done = bf16[512,1,2,4096]{3,0,2,1:T(8,128)(2,1)} async-done(((bf16[512,1,2,512]{3,0,2,1:T(8,128)(2,1)}), bf16[512,1,2,4096]{3,0,2,1:T(8,128)(2,1)}) %all-gather.5.cloned.1.call-update) | async-done | bytes 8388624 | tf_op jit(solution)/shard_map/all_gather | solution.py:47
  203.3 12.0 %copy.52 = bf16[512,1,2,4096]{0,3,2,1:T(8,128)(2,1)} copy(bf16[512,1,2,4096]{3,0,2,1:T(8,128)(2,1)} %all-gather.5.cloned.1.call-done) | data formatting | bytes 16777216 | tf_op jit(solution)/shard_map/all_gather | solution.py:47
  215.3 17.2 %fusion.4 = f32[512,2048]{1,0:T(8,128)} fusion(bf16[2,2048,4096]{2,1,0:T(8,128)(2,1)} %param.5, bf16[512,8192]{0,1:T(8,128)(2,1)} %bitcast.89), kind=kOutput, calls=%fused_computation.9 | convolution fusion | flops 8589934592 | bytes 25165824 | tf_op jit(solution)/shard_map/dot_general | solution.py:54
  232.5 14.1 %fusion.6 = f32[512,2048]{1,0:T(8,128)} fusion(bf16[2,2048,4096]{2,1,0:T(8,128)(2,1)} %param.5, bf16[512,8192]{0,1:T(8,128)(2,1)S(1)} %bitcast.92), kind=kOutput, calls=%fused_computation.11 | convolution fusion | flops 8589934592 | bytes 25165824 | tf_op jit(solution)/shard_map/dot_general | solution.py:54
  246.6 14.7 %add_convert_fusion.1 = bf16[512,2048]{1,0:T(8,128)(2,1)S(1)} fusion(f32[512,2048]{1,0:T(8,128)} %fusion.4, bf16[2,2048,4096]{2,1,0:T(8,128)(2,1)} %param.5, bf16[512,8192]{0,1:T(8,128)(2,1)} %bitcast.90), kind=kOutput, calls=%fused_computation.33 | convolution fusion | flops 8592031744 | bytes 27262976 | tf_op jit(solution)/shard_map/dot_general | solution.py:54
  261.3 14.3 %subtract_convert_fusion.1 = bf16[512,2048]{1,0:T(8,128)(2,1)S(1)} fusion(f32[512,2048]{1,0:T(8,128)} %fusion.6, bf16[2,2048,4096]{2,1,0:T(8,128)(2,1)} %param.5, bf16[512,8192]{0,1:T(8,128)(2,1)} %bitcast.91), kind=kOutput, calls=%fused_computation.34 | convolution fusion | flops 8592031744 | bytes 27262976 | tf_op jit(solution)/shard_map/dot_general | solution.py:54
  277.9 76.9 %reduce-scatter.7.cloned.1.call-done = bf16[128,4096]{1,0:T(8,128)(2,1)} async-done(((bf16[512,4096]{1,0:T(8,128)(2,1)}), bf16[128,4096]{1,0:T(8,128)(2,1)}) %reduce-scatter.7.cloned.1.call-update) | async-done | bytes 1048592 | tf_op jit(solution)/shard_map/reduce_scatter | solution.py:58
  359.9 54.8 %all-gather.7.cloned.1.call-done = bf16[128,2,16384]{0,1,2:T(2,128)(2,1)} async-done(((bf16[128,2,2048]{0,1,2:T(2,128)(2,1)}), bf16[128,2,16384]{0,1,2:T(2,128)(2,1)}) %all-gather.7.cloned.1.call-update) | async-done | bytes 8388624 | tf_op jit(solution)/shard_map/all_gather | solution.py:65
  428.3 15.8 %scatter_custom_fusion.1 = bf16[128,32768]{0,1:T(8,128)(2,1)} fusion(s32[4096]{0:T(1024)S(1)} %bitcast.109, bf16[4096,128]{1,0:T(8,128)(2,1)S(1)} %bitcast.102, bf16[]{:T(256)} %constant.36.clone.1), kind=kCustom, calls=%fused_computation.35 | custom fusion | bytes 8388610 | tf_op jit(solution)/shard_map/scatter | solution.py:41
  444.1 11.6 %copy.58 = bf16[128,4,2,4096]{3,0,2,1:T(8,128)(2,1)} copy(bf16[128,4,2,4096]{0,3,2,1:T(8,128)(2,1)} %bitcast.87) | data formatting | bytes 16777216 | tf_op jit(solution)/shard_map/reshape | solution.py:42
  455.8 71.4 %reduce-scatter.9.cloned.1.call-done = bf16[128,4,2,512]{3,0,2,1:T(8,128)(2,1)} async-done(((bf16[128,4,2,4096]{3,0,2,1:T(8,128)(2,1)}), bf16[128,4,2,512]{3,0,2,1:T(8,128)(2,1)}) %reduce-scatter.9.cloned.1.call-update) | async-done | bytes 1048592 | tf_op jit(solution)/shard_map/reduce_scatter | solution.py:43
  527.2 30.2 %all_to_all.37 = bf16[128,4,2,512]{3,0,2,1:T(8,128)(2,1)S(1)} all-to-all(bf16[128,4,2,512]{3,0,2,1:T(8,128)(2,1)} %reduce-scatter.9.cloned.1.call-done), channel_id=1, replica_groups=mesh['tile'=8,'col'=4] {'col'}, dimensions={1} | all-to-all | bytes 2097152 | tf_op jit(solution)/shard_map/all_to_all | solution.py:46
  558.5 54.1 %all-gather.9.cloned.1.call-done = bf16[512,1,2,4096]{3,0,2,1:T(8,128)(2,1)} async-done(((bf16[512,1,2,512]{3,0,2,1:T(8,128)(2,1)}), bf16[512,1,2,4096]{3,0,2,1:T(8,128)(2,1)}) %all-gather.9.cloned.1.call-update) | async-done | bytes 8388624 | tf_op jit(solution)/shard_map/all_gather | solution.py:47
  612.6 12.2 %copy.60 = bf16[512,1,2,4096]{0,3,2,1:T(8,128)(2,1)} copy(bf16[512,1,2,4096]{3,0,2,1:T(8,128)(2,1)} %all-gather.9.cloned.1.call-done) | data formatting | bytes 16777216 | tf_op jit(solution)/shard_map/all_gather | solution.py:47
  624.9 17.2 %fusion = f32[512,2048]{1,0:T(8,128)} fusion(bf16[2,2048,4096]{2,1,0:T(8,128)(2,1)} %param.5, bf16[512,8192]{0,1:T(8,128)(2,1)} %bitcast.93), kind=kOutput, calls=%fused_computation.5 | convolution fusion | flops 8589934592 | bytes 25165824 | tf_op jit(solution)/shard_map/dot_general | solution.py:54
  642.1 14.1 %fusion.2 = f32[512,2048]{1,0:T(8,128)} fusion(bf16[2,2048,4096]{2,1,0:T(8,128)(2,1)} %param.5, bf16[512,8192]{0,1:T(8,128)(2,1)S(1)} %bitcast.96), kind=kOutput, calls=%fused_computation.7 | convolution fusion | flops 8589934592 | bytes 25165824 | tf_op jit(solution)/shard_map/dot_general | solution.py:54
  656.1 14.6 %add_convert_fusion = bf16[512,2048]{1,0:T(8,128)(2,1)S(1)} fusion(f32[512,2048]{1,0:T(8,128)} %fusion, bf16[2,2048,4096]{2,1,0:T(8,128)(2,1)} %param.5, bf16[512,8192]{0,1:T(8,128)(2,1)} %bitcast.94), kind=kOutput, calls=%fused_computation.31 | convolution fusion | flops 8592031744 | bytes 27262976 | tf_op jit(solution)/shard_map/dot_general | solution.py:54
  670.7 14.3 %subtract_convert_fusion = bf16[512,2048]{1,0:T(8,128)(2,1)S(1)} fusion(f32[512,2048]{1,0:T(8,128)} %fusion.2, bf16[2,2048,4096]{2,1,0:T(8,128)(2,1)} %param.5, bf16[512,8192]{0,1:T(8,128)(2,1)} %bitcast.95), kind=kOutput, calls=%fused_computation.32 | convolution fusion | flops 8592031744 | bytes 27262976 | tf_op jit(solution)/shard_map/dot_general | solution.py:54
  687.3 76.9 %reduce-scatter.11.cloned.1.call-done = bf16[128,4096]{1,0:T(8,128)(2,1)} async-done(((bf16[512,4096]{1,0:T(8,128)(2,1)}), bf16[128,4096]{1,0:T(8,128)(2,1)}) %reduce-scatter.11.cloned.1.call-update) | async-done | bytes 1048592 | tf_op jit(solution)/shard_map/reduce_scatter | solution.py:58
  769.5 54.9 %all-gather.11.cloned.1.call-done = bf16[128,2,16384]{0,1,2:T(2,128)(2,1)} async-done(((bf16[128,2,2048]{0,1,2:T(2,128)(2,1)}), bf16[128,2,16384]{0,1,2:T(2,128)(2,1)}) %all-gather.11.cloned.1.call-update) | async-done | bytes 8388624 | tf_op jit(solution)/shard_map/all_gather | solution.py:65
  (77 shorter events, 55.1 us)
Async XLA Ops:
  7.2 6.1 copy-start.3
  7.2 110.7 %reduce-scatter.5.cloned.1.call-start = ((), (), s32[]{:S(2)}) async-start(), calls=%async_computation.6 | async-start | bytes 9437184 | tf_op jit(solution)/shard_map/reduce_scatter | solution.py:43
  8.6 7.6 copy-start.4
  11.0 5.3 copy-start.7
  43.7 159.6 %all-gather.5.cloned.1.call-start = ((), (), s32[]{:S(2)}) async-start(), calls=%async_computation.7 | async-start | bytes 9437184 | tf_op jit(solution)/shard_map/all_gather | solution.py:47
  149.1 205.7 %reduce-scatter.7.cloned.1.call-start = ((), (), s32[]{:S(2)}) async-start(), calls=%async_computation.8 | async-start | bytes 5242880 | tf_op jit(solution)/shard_map/reduce_scatter | solution.py:58
  215.3 17.2 %copy-start = (bf16[512,1,2,4096]{0,3,2,1:T(8,128)(2,1)S(1)}, bf16[512,1,2,4096]{0,3,2,1:T(8,128)(2,1)}, u32[]{:S(2)}) copy-start(bf16[512,1,2,4096]{0,3,2,1:T(8,128)(2,1)} %copy.52) | copy-start | bytes 25165828
  277.9 136.8 %all-gather.7.cloned.1.call-start = ((), (), s32[]{:S(2)}) async-start(), calls=%async_computation.9 | async-start | bytes 9437184 | tf_op jit(solution)/shard_map/all_gather | solution.py:65
  359.8 167.5 %reduce-scatter.9.cloned.1.call-start = ((), (), s32[]{:S(2)}) async-start(), calls=%async_computation.10 | async-start | bytes 9437184 | tf_op jit(solution)/shard_map/reduce_scatter | solution.py:43
  426.2 1.0 copy-start.5
  426.2 1.2 copy-start.8
  426.2 1.3 copy-start.10
  455.8 156.9 %all-gather.9.cloned.1.call-start = ((), (), s32[]{:S(2)}) async-start(), calls=%async_computation.11 | async-start | bytes 9437184 | tf_op jit(solution)/shard_map/all_gather | solution.py:47
  558.5 205.8 %reduce-scatter.11.cloned.1.call-start = ((), (), s32[]{:S(2)}) async-start(), calls=%async_computation.12 | async-start | bytes 5242880 | tf_op jit(solution)/shard_map/reduce_scatter | solution.py:58
  624.9 17.2 %copy-start.1 = (bf16[512,1,2,4096]{0,3,2,1:T(8,128)(2,1)S(1)}, bf16[512,1,2,4096]{0,3,2,1:T(8,128)(2,1)}, u32[]{:S(2)}) copy-start(bf16[512,1,2,4096]{0,3,2,1:T(8,128)(2,1)} %copy.60) | copy-start | bytes 25165828
  687.3 137.1 %all-gather.11.cloned.1.call-start = ((), (), s32[]{:S(2)}) async-start(), calls=%async_computation.13 | async-start | bytes 9437184 | tf_op jit(solution)/shard_map/all_gather | solution.py:65
  766.4 69.2 %copy-start.2 = (bf16[128,2,2048]{2,1,0:T(2,128)(2,1)}, bf16[128,2,2048]{2,1,0:T(2,128)(2,1)S(1)}, u32[]{:S(2)}) copy-start(bf16[128,2,2048]{2,1,0:T(2,128)(2,1)S(1)} %reshape.165) | copy-start | bytes 3145732
  835.7 1.0 copy-start.6
  835.8 1.2 copy-start.9
  835.8 1.3 copy-start.11
Sparse Core Ops, SparseCore 0:
  43.8 73.9 reduce-scatter.4
  149.2 53.9 all-gather.4
  278.0 76.7 reduce-scatter.6
  359.9 54.7 all-gather.6
  455.9 71.2 reduce-scatter.8
  558.6 53.9 all-gather.8
  687.4 76.7 reduce-scatter.10
  769.6 54.7 all-gather.10
where the time goes:
time: 855 us; the launch traced here: 847 us
  waiting for transfers between devices  517 us (60%)
  matrix products  124 us (15%)
  local copies, waits for them, and re-layouts  121 us (14%)
  blocking collectives  60.3 us (7%)
  between operations  15 us (2%)
  other arithmetic  8.68 us (1%)
    reduce_scatter x2, waiting for transfers between devices, per_device(): lax.psum_scatter(jnp.concatenate([real_part, imag_part], 1).astype(jnp.bf...  154 us
    reduce_scatter x2, waiting for transfers between devices, per_device(): lax.psum_scatter(placed.astype(jnp.float32).astype(jnp.bfloat16), 'tile',...  146 us
    dot_general x8, matrix products, dot_rows(): lax.dot_general(left, right, contract, preferred_element_type=jnp.float32)  121 us
    all_gather x2, waiting for transfers between devices, per_device(): gathered = lax.all_gather(pressure, 'tile', axis=2, tiled=True)  110 us
    all_gather x2, waiting for transfers between devices, per_device(): full_cols = lax.all_gather(moved, 'tile', axis=3, tiled=True)  108 us
    all_to_all x2, blocking collectives, per_device(): lax.all_to_all(shares, 'col', split_axis=1, concat_axis=0, tiled=True)  60.3 us
    scatter x2, local copies, waits for them, and re-layouts, per_device(): jnp.zeros((loads_dev, 2 * patch_count), jnp.bfloat16).at[:, flat_index]  31.5 us
    all_gather x2, local copies, waits for them, and re-layouts, per_device(): full_cols = lax.all_gather(moved, 'tile', axis=3, tiled=True)  24.2 us
  transfers between devices with their start and end apart: 8, of which 8 were waited for; matrix products, arithmetic and copies ran while one was open for 0% of the time, Pallas kernels for 0%

commit v1 on v0

--- a/solution.py
+++ b/solution.py
@@ -43,7 +43,15 @@
         shares = lax.psum_scatter(
             placed.astype(jnp.float32).astype(jnp.bfloat16), "tile", scatter_dimension=3, tiled=True
         )
-        moved = lax.all_to_all(shares, "col", split_axis=1, concat_axis=0, tiled=True)
+        ways, here = (lax.axis_size("col"), lax.axis_index("col"))
+        width = shares.shape[1] // ways
+        turned = jnp.roll(shares, -here * width, axis=1)
+        got = [lax.slice_in_dim(turned, 0, width, axis=1)]
+        for far in range(1, ways):
+            sent = lax.slice_in_dim(turned, far * width, (far + 1) * width, axis=1)
+            got.append(lax.ppermute(sent, "col", [(d, (d + far) % ways) for d in range(ways)]))
+        line = jnp.concatenate(got[::-1], axis=0)
+        moved = jnp.roll(line, (here + 1) * got[0].shape[0], axis=0)
         full_cols = lax.all_gather(moved, "tile", axis=3, tiled=True)
         columns = full_cols.reshape(full_cols.shape[0], 2 * col_width)
         vel_re = columns[:, :col_width]

time: 855 us -> 802 us (0.938)
  blocking collectives: 60.3 us -> 0 us
  local copies, waits for them, and re-layouts: 121 us -> 72.5 us
  waiting for transfers between devices: 517 us -> 557 us
  starting transfers between devices: 0.54 us -> 11.2 us
    all_to_all x2 -> x0, blocking collectives: 60.3 us -> none  [per_device(): lax.all_to_all(shares, 'col', split_axis=1, concat_axis=0, tiled=True)]
    ppermute x0 -> x6, waiting for transfers between devices: none -> 31.7 us  [per_device(): lax.ppermute(sent, 'col', [(d, (d + far) % ways) for d in range(ways)])]
    all_gather x2 -> x0, local copies, waits for them, and re-layouts: 24.2 us -> none  [per_device(): full_cols = lax.all_gather(moved, 'tile', axis=3, tiled=True)]
    reshape x2 -> x0, local copies, waits for them, and re-layouts: 23.3 us -> none  [per_device(): placed = placed.reshape(loads_dev, col_tiles, 2, col_width)]
    ppermute x0 -> x6, starting transfers between devices: none -> 10.6 us  [per_device(): lax.ppermute(sent, 'col', [(d, (d + far) % ways) for d in range(ways)])]
  transfers between devices with their start and end apart: 8 -> 14, of which waited for: 8 -> 12; matrix products, arithmetic and copies ran while one was open for 0% -> 0% of each run, Pallas kernels for 0% -> 0%
where the time goes in v1:
time: 802 us; the launch traced here: 794 us
  waiting for transfers between devices  557 us (69%)
  matrix products  123 us (15%)
  local copies, waits for them, and re-layouts  72.5 us (9%)
  other arithmetic  16.4 us (2%)
  between operations  15 us (2%)
  starting transfers between devices  11.2 us (1%)
    reduce_scatter x2, waiting for transfers between devices, per_device(): lax.psum_scatter(jnp.concatenate([real_part, imag_part], 1).astype(jnp.bf...  154 us
    reduce_scatter x2, waiting for transfers between devices, per_device(): lax.psum_scatter(placed.astype(jnp.float32).astype(jnp.bfloat16), 'tile',...  146 us
    dot_general x8, matrix products, dot_rows(): lax.dot_general(left, right, contract, preferred_element_type=jnp.float32)  119 us
    all_gather x2, waiting for transfers between devices, per_device(): full_cols = lax.all_gather(moved, 'tile', axis=3, tiled=True)  116 us
    all_gather x2, waiting for transfers between devices, per_device(): gathered = lax.all_gather(pressure, 'tile', axis=2, tiled=True)  110 us
    ppermute x6, waiting for transfers between devices, per_device(): lax.ppermute(sent, 'col', [(d, (d + far) % ways) for d in range(ways)])  31.7 us
    scatter x2, local copies, waits for them, and re-layouts, per_device(): jnp.zeros((loads_dev, 2 * patch_count), jnp.bfloat16).at[:, flat_index]  31.6 us
    gather x2, local copies, waits for them, and re-layouts, per_device(): gathered[:, :, slot_flat].reshape(loads_dev, 2, slot_count, panel_width)  21 us
  transfers between devices with their start and end apart: 14, of which 12 were waited for; matrix products, arithmetic and copies ran while one was open for 0% of the time, Pallas kernels for 0%

profile of v1, /device:TPU:0, one launch (start us, length us, event | category | flops | bytes accessed | tf_op | source)
XLA Modules:
  0.0 794.4 jit_solution(9934938635551782630)
XLA Ops:
  16.2 15.8 %scatter_custom_fusion = bf16[128,32768]{0,1:T(8,128)(2,1)} fusion(s32[4096]{0:T(1024)S(1)} %bitcast.88, bf16[4096,128]{1,0:T(8,128)(2,1)S(1)} %bitcast.81, bf16[]{:T(256)} %constant.73.clone.1), kind=kCustom, calls=%fused_computation.37 | custom fusion | bytes 8388610 | tf_op jit(solution)/shard_map/scatter | solution.py:41
  32.2 74.2 %reduce-scatter.5.cloned.1.call-done = bf16[128,4,2,512]{0,3,2,1:T(8,128)(2,1)} async-done(((bf16[128,4,2,4096]{0,3,2,1:T(8,128)(2,1)}), bf16[128,4,2,512]{0,3,2,1:T(8,128)(2,1)}) %reduce-scatter.5.cloned.1.call-update) | async-done | bytes 1048592 | tf_op jit(solution)/shard_map/reduce_scatter | solution.py:43
  114.1 6.0 collective-permute-done.2
  120.2 9.9 %collective-permute-done.1 = bf16[128,1,2,512]{0,3,2,1:T(8,128)(2,1)S(1)} collective-permute-done((bf16[128,1,2,512]{0,3,2,1:T(8,128)(2,1)}, bf16[128,1,2,512]{0,3,2,1:T(8,128)(2,1)S(1)}, u32[]{:S(2)}, u32[]{:S(2)}) %collective-permute-start.1) | collective-permute-done | bytes 262176 | tf_op jit(solution)/shard_map/ppermute | solution.py:52
  132.6 57.8 %all-gather.5.cloned.1.call-done = bf16[512,1,2,4096]{0,3,2,1:T(8,128)(2,1)} async-done(((bf16[512,1,2,512]{0,3,2,1:T(8,128)(2,1)}), bf16[512,1,2,4096]{0,3,2,1:T(8,128)(2,1)}) %all-gather.5.cloned.1.call-update) | async-done | bytes 8388624 | tf_op jit(solution)/shard_map/all_gather | solution.py:55
  190.4 15.0 %fusion.4 = f32[512,2048]{1,0:T(8,128)} fusion(bf16[2,2048,4096]{2,1,0:T(8,128)(2,1)} %param.9, bf16[512,8192]{0,1:T(8,128)(2,1)} %bitcast.90), kind=kOutput, calls=%fused_computation.9 | convolution fusion | flops 8589934592 | bytes 25165824 | tf_op jit(solution)/shard_map/dot_general | solution.py:62
  205.4 15.0 %fusion.6 = f32[512,2048]{1,0:T(8,128)} fusion(bf16[2,2048,4096]{2,1,0:T(8,128)(2,1)} %param.9, bf16[512,8192]{0,1:T(8,128)(2,1)} %bitcast.91), kind=kOutput, calls=%fused_computation.11 | convolution fusion | flops 8589934592 | bytes 25165824 | tf_op jit(solution)/shard_map/dot_general | solution.py:62
  220.4 14.7 %add_convert_fusion.1 = bf16[512,2048]{1,0:T(8,128)(2,1)S(1)} fusion(f32[512,2048]{1,0:T(8,128)} %fusion.4, bf16[2,2048,4096]{2,1,0:T(8,128)(2,1)} %param.9, bf16[512,8192]{0,1:T(8,128)(2,1)} %bitcast.92), kind=kOutput, calls=%fused_computation.33 | convolution fusion | flops 8592031744 | bytes 27262976 | tf_op jit(solution)/shard_map/dot_general | solution.py:62
  235.2 14.3 %subtract_convert_fusion.1 = bf16[512,2048]{1,0:T(8,128)(2,1)S(1)} fusion(f32[512,2048]{1,0:T(8,128)} %fusion.6, bf16[2,2048,4096]{2,1,0:T(8,128)(2,1)} %param.9, bf16[512,8192]{0,1:T(8,128)(2,1)} %bitcast.93), kind=kOutput, calls=%fused_computation.34 | convolution fusion | flops 8592031744 | bytes 27262976 | tf_op jit(solution)/shard_map/dot_general | solution.py:62
  251.8 76.9 %reduce-scatter.7.cloned.1.call-done = bf16[128,4096]{1,0:T(8,128)(2,1)} async-done(((bf16[512,4096]{1,0:T(8,128)(2,1)}), bf16[128,4096]{1,0:T(8,128)(2,1)}) %reduce-scatter.7.cloned.1.call-update) | async-done | bytes 1048592 | tf_op jit(solution)/shard_map/reduce_scatter | solution.py:66
  333.8 54.8 %all-gather.7.cloned.1.call-done = bf16[128,2,16384]{0,1,2:T(2,128)(2,1)} async-done(((bf16[128,2,2048]{0,1,2:T(2,128)(2,1)}), bf16[128,2,16384]{0,1,2:T(2,128)(2,1)}) %all-gather.7.cloned.1.call-update) | async-done | bytes 8388624 | tf_op jit(solution)/shard_map/all_gather | solution.py:73
  388.6 10.6 %gather_fusion.1 = bf16[2048,128,2]{1,2,0:T(2,128)(2,1)S(1)} fusion(bf16[128,2,16384]{0,1,2:T(2,128)(2,1)} %all-gather.7.cloned.1.call-done, s32[2048]{0:T(1024)S(1)} %broadcast_clamp_fusion), kind=kCustom, calls=%fused_computation.1 | custom fusion | bytes 2105344 | tf_op jit(solution)/shard_map/gather | solution.py:75
  401.9 15.8 %scatter_custom_fusion.1 = bf16[128,32768]{0,1:T(8,128)(2,1)} fusion(s32[4096]{0:T(1024)S(1)} %bitcast.89, bf16[4096,128]{1,0:T(8,128)(2,1)S(1)} %bitcast.82, bf16[]{:T(256)} %constant.73.clone.1), kind=kCustom, calls=%fused_computation.35 | custom fusion | bytes 8388610 | tf_op jit(solution)/shard_map/scatter | solution.py:41
  417.8 71.5 %reduce-scatter.9.cloned.1.call-done = bf16[128,4,2,512]{0,3,2,1:T(8,128)(2,1)} async-done(((bf16[128,4,2,4096]{0,3,2,1:T(8,128)(2,1)}), bf16[128,4,2,512]{0,3,2,1:T(8,128)(2,1)}) %reduce-scatter.9.cloned.1.call-update) | async-done | bytes 1048592 | tf_op jit(solution)/shard_map/reduce_scatter | solution.py:43
  496.3 5.8 collective-permute-done.5
  502.1 9.9 %collective-permute-done.4 = bf16[128,1,2,512]{0,3,2,1:T(8,128)(2,1)S(1)} collective-permute-done((bf16[128,1,2,512]{0,3,2,1:T(8,128)(2,1)S(1)}, bf16[128,1,2,512]{0,3,2,1:T(8,128)(2,1)S(1)}, u32[]{:S(2)}, u32[]{:S(2)}) %collective-permute-start.4) | collective-permute-done | bytes 262176 | tf_op jit(solution)/shard_map/ppermute | solution.py:52
  514.4 58.0 %all-gather.9.cloned.1.call-done = bf16[512,1,2,4096]{0,3,2,1:T(8,128)(2,1)} async-done(((bf16[512,1,2,512]{0,3,2,1:T(8,128)(2,1)}), bf16[512,1,2,4096]{0,3,2,1:T(8,128)(2,1)}) %all-gather.9.cloned.1.call-update) | async-done | bytes 8388624 | tf_op jit(solution)/shard_map/all_gather | solution.py:55
  572.4 17.3 %fusion = f32[512,2048]{1,0:T(8,128)} fusion(bf16[2,2048,4096]{2,1,0:T(8,128)(2,1)} %param.9, bf16[512,8192]{0,1:T(8,128)(2,1)} %bitcast.94), kind=kOutput, calls=%fused_computation.5 | convolution fusion | flops 8589934592 | bytes 25165824 | tf_op jit(solution)/shard_map/dot_general | solution.py:62
  589.7 14.0 %fusion.2 = f32[512,2048]{1,0:T(8,128)} fusion(bf16[2,2048,4096]{2,1,0:T(8,128)(2,1)} %param.9, bf16[512,8192]{0,1:T(8,128)(2,1)S(1)} %bitcast.97), kind=kOutput, calls=%fused_computation.7 | convolution fusion | flops 8589934592 | bytes 25165824 | tf_op jit(solution)/shard_map/dot_general | solution.py:62
  603.7 14.6 %add_convert_fusion = bf16[512,2048]{1,0:T(8,128)(2,1)S(1)} fusion(f32[512,2048]{1,0:T(8,128)} %fusion, bf16[2,2048,4096]{2,1,0:T(8,128)(2,1)} %param.9, bf16[512,8192]{0,1:T(8,128)(2,1)} %bitcast.95), kind=kOutput, calls=%fused_computation.31 | convolution fusion | flops 8592031744 | bytes 27262976 | tf_op jit(solution)/shard_map/dot_general | solution.py:62
  618.3 14.3 %subtract_convert_fusion = bf16[512,2048]{1,0:T(8,128)(2,1)S(1)} fusion(f32[512,2048]{1,0:T(8,128)} %fusion.2, bf16[2,2048,4096]{2,1,0:T(8,128)(2,1)} %param.9, bf16[512,8192]{0,1:T(8,128)(2,1)} %bitcast.96), kind=kOutput, calls=%fused_computation.32 | convolution fusion | flops 8592031744 | bytes 27262976 | tf_op jit(solution)/shard_map/dot_general | solution.py:62
  634.9 76.9 %reduce-scatter.11.cloned.1.call-done = bf16[128,4096]{1,0:T(8,128)(2,1)} async-done(((bf16[512,4096]{1,0:T(8,128)(2,1)}), bf16[128,4096]{1,0:T(8,128)(2,1)}) %reduce-scatter.11.cloned.1.call-update) | async-done | bytes 1048592 | tf_op jit(solution)/shard_map/reduce_scatter | solution.py:66
  717.0 54.9 %all-gather.11.cloned.1.call-done = bf16[128,2,16384]{0,1,2:T(2,128)(2,1)} async-done(((bf16[128,2,2048]{0,1,2:T(2,128)(2,1)}), bf16[128,2,16384]{0,1,2:T(2,128)(2,1)}) %all-gather.11.cloned.1.call-update) | async-done | bytes 8388624 | tf_op jit(solution)/shard_map/all_gather | solution.py:73
  771.9 10.4 %gather_fusion.2 = bf16[2048,128,2]{1,2,0:T(2,128)(2,1)S(1)} fusion(bf16[128,2,16384]{0,1,2:T(2,128)(2,1)} %all-gather.11.cloned.1.call-done, s32[2048]{0:T(1024)S(1)} %broadcast_clamp_fusion), kind=kCustom, calls=%fused_computation.2 | custom fusion | bytes 2105344 | tf_op jit(solution)/shard_map/gather | solution.py:75
  (81 shorter events, 50.9 us)
Async XLA Ops:
  7.2 6.1 copy-start.1
  7.2 99.2 %reduce-scatter.5.cloned.1.call-start = ((), (), s32[]{:S(2)}) async-start(), calls=%async_computation.4 | async-start | bytes 9437184 | tf_op jit(solution)/shard_map/reduce_scatter | solution.py:43
  8.6 392.1 %copy-start.2 = (bf16[32,64,64]{1,2,0:T(8,128)(2,1)}, bf16[32,64,64]{1,2,0:T(8,128)(2,1)S(1)}, u32[]{:S(2)}) copy-start(bf16[32,64,64]{1,2,0:T(8,128)(2,1)S(1)} %fusion.77) | copy-start | bytes 786436
  11.0 389.7 %copy-start.4 = (bf16[32,64,64]{1,2,0:T(8,128)(2,1)}, bf16[32,64,64]{1,2,0:T(8,128)(2,1)S(1)}, u32[]{:S(2)}) copy-start(bf16[32,64,64]{1,2,0:T(8,128)(2,1)S(1)} %get-tuple-element.20) | copy-start | bytes 786436
  32.1 158.3 %all-gather.5.cloned.1.call-start = ((), (), s32[]{:S(2)}) async-start(), calls=%async_computation.5 | async-start | bytes 9437184 | tf_op jit(solution)/shard_map/all_gather | solution.py:55
  108.8 11.3 %collective-permute-start.2 = (bf16[128,1,2,512]{0,3,2,1:T(8,128)(2,1)}, bf16[128,1,2,512]{0,3,2,1:T(8,128)(2,1)S(1)}, u32[]{:S(2)}, u32[]{:S(2)}) collective-permute-start(bf16[128,1,2,512]{0,3,2,1:T(8,128)(2,1)} %get-tuple-element.17), channel_id=1, source_target_pairs={{0,1},{1,2},{2,3},{3,0},{4,5},{5,6},{6,7},{7,4},{8,9},{9,10},{10,1... | collective-permute-start | bytes 786440 | tf_op jit(solution)/shard_map/ppermute | solution.py:52
  110.3 19.8 %collective-permute-start.1 = (bf16[128,1,2,512]{0,3,2,1:T(8,128)(2,1)}, bf16[128,1,2,512]{0,3,2,1:T(8,128)(2,1)S(1)}, u32[]{:S(2)}, u32[]{:S(2)}) collective-permute-start(bf16[128,1,2,512]{0,3,2,1:T(8,128)(2,1)} %get-tuple-element.18), channel_id=1, source_target_pairs={{0,2},{1,3},{2,0},{3,1},{4,6},{5,7},{6,4},{7,5},{8,10},{9,11},{10,... | collective-permute-start | bytes 786440 | tf_op jit(solution)/shard_map/ppermute | solution.py:52
  112.7 17.4 %collective-permute-start = (bf16[128,1,2,512]{0,3,2,1:T(8,128)(2,1)S(1)}, bf16[128,1,2,512]{0,3,2,1:T(8,128)(2,1)S(1)}, u32[]{:S(2)}, u32[]{:S(2)}) collective-permute-start(bf16[128,1,2,512]{0,3,2,1:T(8,128)(2,1)S(1)} %get-tuple-element.19), channel_id=1, source_target_pairs={{0,3},{1,0},{2,1},{3,2},{4,7},{5,4},{6,5},{7,6},{8,11},{9,8},{10,9... | collective-permute-start | bytes 786440 | tf_op jit(solution)/shard_map/ppermute | solution.py:52
  132.4 196.3 %reduce-scatter.7.cloned.1.call-start = ((), (), s32[]{:S(2)}) async-start(), calls=%async_computation.6 | async-start | bytes 5242880 | tf_op jit(solution)/shard_map/reduce_scatter | solution.py:66
  251.8 136.8 %all-gather.7.cloned.1.call-start = ((), (), s32[]{:S(2)}) async-start(), calls=%async_computation.7 | async-start | bytes 9437184 | tf_op jit(solution)/shard_map/all_gather | solution.py:73
  333.6 155.7 %reduce-scatter.9.cloned.1.call-start = ((), (), s32[]{:S(2)}) async-start(), calls=%async_computation.8 | async-start | bytes 9437184 | tf_op jit(solution)/shard_map/reduce_scatter | solution.py:43
  400.1 1.0 copy-start.6
  417.7 154.7 %all-gather.9.cloned.1.call-start = ((), (), s32[]{:S(2)}) async-start(), calls=%async_computation.9 | async-start | bytes 9437184 | tf_op jit(solution)/shard_map/all_gather | solution.py:55
  491.0 11.2 %collective-permute-start.5 = (bf16[128,1,2,512]{0,3,2,1:T(8,128)(2,1)S(1)}, bf16[128,1,2,512]{0,3,2,1:T(8,128)(2,1)S(1)}, u32[]{:S(2)}, u32[]{:S(2)}) collective-permute-start(bf16[128,1,2,512]{0,3,2,1:T(8,128)(2,1)S(1)} %get-tuple-element.13), channel_id=1, source_target_pairs={{0,1},{1,2},{2,3},{3,0},{4,5},{5,6},{6,7},{7,4},{8,9},{9,10},{10,1... | collective-permute-start | bytes 786440 | tf_op jit(solution)/shard_map/ppermute | solution.py:52
  492.5 19.6 %collective-permute-start.4 = (bf16[128,1,2,512]{0,3,2,1:T(8,128)(2,1)S(1)}, bf16[128,1,2,512]{0,3,2,1:T(8,128)(2,1)S(1)}, u32[]{:S(2)}, u32[]{:S(2)}) collective-permute-start(bf16[128,1,2,512]{0,3,2,1:T(8,128)(2,1)S(1)} %get-tuple-element.14), channel_id=1, source_target_pairs={{0,2},{1,3},{2,0},{3,1},{4,6},{5,7},{6,4},{7,5},{8,10},{9,11},{10,... | collective-permute-start | bytes 786440 | tf_op jit(solution)/shard_map/ppermute | solution.py:52
  494.9 17.2 %collective-permute-start.3 = (bf16[128,1,2,512]{0,3,2,1:T(8,128)(2,1)S(1)}, bf16[128,1,2,512]{0,3,2,1:T(8,128)(2,1)S(1)}, u32[]{:S(2)}, u32[]{:S(2)}) collective-permute-start(bf16[128,1,2,512]{0,3,2,1:T(8,128)(2,1)S(1)} %get-tuple-element.15), channel_id=1, source_target_pairs={{0,3},{1,0},{2,1},{3,2},{4,7},{5,4},{6,5},{7,6},{8,11},{9,8},{10,9... | collective-permute-start | bytes 786440 | tf_op jit(solution)/shard_map/ppermute | solution.py:52
  514.4 197.5 %reduce-scatter.11.cloned.1.call-start = ((), (), s32[]{:S(2)}) async-start(), calls=%async_computation.10 | async-start | bytes 5242880 | tf_op jit(solution)/shard_map/reduce_scatter | solution.py:66
  572.4 17.3 %copy-start.8 = (bf16[512,1,2,4096]{0,3,2,1:T(8,128)(2,1)S(1)}, bf16[512,1,2,4096]{0,3,2,1:T(8,128)(2,1)}, u32[]{:S(2)}) copy-start(bf16[512,1,2,4096]{0,3,2,1:T(8,128)(2,1)} %all-gather.9.cloned.1.call-done) | copy-start | bytes 25165828
  634.9 137.1 %all-gather.11.cloned.1.call-start = ((), (), s32[]{:S(2)}) async-start(), calls=%async_computation.11 | async-start | bytes 9437184 | tf_op jit(solution)/shard_map/all_gather | solution.py:73
  713.9 69.2 %copy-start = (bf16[128,2,2048]{2,1,0:T(2,128)(2,1)}, bf16[128,2,2048]{2,1,0:T(2,128)(2,1)S(1)}, u32[]{:S(2)}) copy-start(bf16[128,2,2048]{2,1,0:T(2,128)(2,1)S(1)} %reshape.165) | copy-start | bytes 3145732
  783.3 1.0 copy-start.3
  783.3 1.2 copy-start.5
  783.3 1.3 copy-start.7
Sparse Core Ops, SparseCore 0:
  32.2 74.1 reduce-scatter.4
  132.5 57.8 all-gather.4
  251.9 76.7 reduce-scatter.6
  333.7 54.7 all-gather.6
  417.9 71.3 reduce-scatter.8
  514.5 57.8 all-gather.8
  635.0 76.7 reduce-scatter.10
  717.2 54.7 all-gather.10
